TPU v7x, 256 devices: a whole 4x4x8 slice. The times are simulated.
256 devices in a mesh: batch: 128 (over y, z, x_lo, core), span: 2 (over x_hi).
Axes of the slice: x: 4 (x_hi: 2, x_lo: 2; x = x_hi * 2 + x_lo), y: 4, z: 8, core: 2. Of those that a mesh axis runs over, the one named last changes fastest.
Arguments:
- image_tokens: bfloat16 [256, 256, 512], P('batch'), may hold values from -400 to 400
- captions: bfloat16 [2048, 512], P(('batch', 'span')), may hold values from -6 to 6
- owner: int32 [2048], P(('batch', 'span')), may hold values from 0 to 255
- w_query: bfloat16 [512, 512], replicated, may hold values from -0.25 to 0.25
- w_key: bfloat16 [512, 512], replicated, may hold values from -0.25 to 0.25
- w_value: bfloat16 [512, 512], replicated, may hold values from -0.25 to 0.25
- w_out: bfloat16 [512, 512], replicated, may hold values from -0.25 to 0.25
Outputs:
- caption_grad: float32 [2048, 512], P(('batch', 'span'))
- token_grad: float32 [256, 256, 512], P('batch')
Inputs may be any that keep to these rules, and one draw needn't show every extreme that they name: `owner`: each caption names one image.
All inputs are finite; a program needn't handle non-finite values.
Results may differ from a plain program's by a relative error of at most 0.039.
The roundings to bfloat16 on the way count: a program that leaves them out, or rounds other values in their place, can miss the bound.
Values may be sent and summed in bfloat16 or wider, within the bound.
No kernel may reach another device: no remote copies, remote signals or barrier semaphores. Data moves between devices by JAX's collectives and lax.ppermute only.
A program may use at most 64 MiB of HBM per device.

v0:
```python
import math

import jax
import jax.numpy as jnp
from jax import lax
from jax.sharding import Mesh
from jax.sharding import PartitionSpec as P

HEADS = 8
HEAD_DIM = 64
D = 512
BATCH = ("batch_0", "batch_1", "batch_2", "batch_3")
BATCH_SPAN = ("batch_0", "batch_1", "batch_2", "batch_3", "span")


LOGIT_SCALE = 10.0
LOGIT_BIAS = -2.0
NORM_EPS = 1e-06


def copy_for_each(x, axis):
    copies = jnp.broadcast_to(x, (lax.axis_size(axis), *x.shape))
    return lax.all_to_all(copies, axis, split_axis=0, concat_axis=0, tiled=True)


def in_order(parts, dim):
    parts = jnp.moveaxis(parts, 0, dim)
    shape = parts.shape
    return parts.reshape(*shape[:dim], shape[dim] * shape[dim + 1], *shape[dim + 2 :])


def whole_of(x, axes, dim):
    far, near = axes
    parts = copy_for_each(copy_for_each(x, far), near)
    return in_order(parts.swapaxes(0, 1).reshape(-1, *x.shape), dim)


def split_up(x, dim, peers):
    before, after = (x.shape[:dim], x.shape[dim + 1 :])
    return jnp.moveaxis(x.reshape(*before, peers, -1, *after), dim, 0)


def summed_on_arrival(x, axis, dim):
    parts = split_up(x, dim, lax.axis_size(axis))
    arrived = lax.all_to_all(parts, axis, split_axis=0, concat_axis=0, tiled=True)
    return arrived.sum(axis=0)


def summed_rows(x, axes, dim):
    far, near = axes
    own = summed_on_arrival(split_up(x, dim, lax.axis_size(far)), near, dim + 1)
    return jnp.sum(lax.all_to_all(own, far, 0, 0, tiled=True), axis=0)


def of_everyone(x, axis):
    return copy_for_each(x, axis).sum(axis=0)


def pair_loss(query, keys, values, caption_f, w_out, owner_block, image_base):
    count = query.shape[0]
    images = keys.shape[0]
    patches = keys.shape[1]
    width = keys.shape[2]
    query_heads = query.reshape(count, HEADS, HEAD_DIM)
    key_heads = keys.reshape(images, patches, HEADS, HEAD_DIM)
    value_heads = values.reshape(images, patches, HEADS, HEAD_DIM)
    scores = jnp.einsum(
        "che,iphe->cihp", query_heads, key_heads, preferred_element_type=jnp.float32
    ) * HEAD_DIM ** (-0.5)
    weights = jax.nn.softmax(scores, axis=-1).astype(jnp.bfloat16)
    pooled = jnp.einsum("cihp,iphe->cihe", weights, value_heads, preferred_element_type=jnp.float32)
    pooled = pooled.reshape(count * images, width).astype(jnp.bfloat16)
    mixed = jnp.dot(pooled, w_out, preferred_element_type=jnp.float32).reshape(count, images, width)
    inner = jnp.sum(mixed * caption_f[:, None, :], axis=-1)
    mixed_norm = jnp.sqrt(jnp.sum(mixed * mixed, axis=-1) + NORM_EPS)
    caption_norm = jnp.sqrt(jnp.sum(caption_f * caption_f, axis=-1) + NORM_EPS)
    cosine = inner / (mixed_norm * caption_norm[:, None])
    logits = LOGIT_SCALE * cosine + LOGIT_BIAS
    image_ids = image_base + jnp.arange(images, dtype=jnp.int32)
    labels = jnp.where(owner_block[:, None] == image_ids[None, :], 1.0, -1.0).astype(jnp.float32)
    return jnp.sum(jax.nn.softplus(-labels * logits))


def process(captions_in, owners_in, keys, values, w_query, w_out, image_base):
    rows = captions_in.shape[0]
    group = math.gcd(rows, 64)
    count = rows // group

    def step(carry, item):
        grad_keys, grad_values = carry
        caption_block, owner_block = item
        query = jnp.dot(caption_block, w_query, preferred_element_type=jnp.float32).astype(
            jnp.bfloat16
        )
        caption_f = caption_block.astype(jnp.float32)

        def local(query_in, keys_in, values_in, caption_in):
            return pair_loss(
                query_in, keys_in, values_in, caption_in, w_out, owner_block, image_base
            )

        value, pull = jax.vjp(local, query, keys, values, caption_f)
        grad_query, more_keys, more_values, grad_direct = pull(jnp.ones((), jnp.float32))
        grads = (grad_direct + jnp.dot(grad_query, w_query.T, preferred_element_type=jnp.float32))[
            None
        ]
        carry = (
            grad_keys + more_keys.astype(jnp.float32),
            grad_values + more_values.astype(jnp.float32),
        )
        return (carry, grads)

    init = (jnp.zeros(keys.shape, jnp.float32), jnp.zeros(values.shape, jnp.float32))
    items = (captions_in.reshape(count, group, D), owners_in.reshape(count, group))
    (grad_keys, grad_values), grads = lax.scan(step, init, items)
    layers = grads.shape[1]
    grads = jnp.transpose(grads, (1, 0, 2, 3)).reshape(layers, rows, D)
    return (grad_keys, grad_values, grads)


def on_device(image_tokens, captions, owner, w_query, w_key, w_value, w_out):
    images = image_tokens.shape[0]
    patches = image_tokens.shape[1]
    token_rows = image_tokens.reshape(images * patches, D)
    keys = (
        jnp.dot(token_rows, w_key, preferred_element_type=jnp.float32)
        .astype(jnp.bfloat16)
        .reshape(images, patches, D)
    )
    values = (
        jnp.dot(token_rows, w_value, preferred_element_type=jnp.float32)
        .astype(jnp.bfloat16)
        .reshape(images, patches, D)
    )
    image_base = lax.axis_index(BATCH) * images
    more_keys, more_values, grads = process(
        whole_of(captions, (("batch_0", "batch_1", "batch_2"), "batch_3"), 0),
        whole_of(owner, (("batch_0", "batch_1", "batch_2"), "batch_3"), 0),
        keys,
        values,
        w_query,
        w_out,
        image_base,
    )
    buffer = grads
    grad_keys, grad_values, buffer = (more_keys, more_values, buffer)
    summed = summed_rows(buffer, (("batch_0", "batch_1", "batch_2"), "batch_3"), 1)
    caption_grad = summed[0]
    caption_grad = 16.0 * caption_grad
    keys_b = grad_keys.reshape(images * patches, D).astype(jnp.bfloat16)
    values_b = grad_values.reshape(images * patches, D).astype(jnp.bfloat16)
    token_part = jnp.dot(keys_b, w_key.T, preferred_element_type=jnp.float32)
    token_part = token_part + jnp.dot(values_b, w_value.T, preferred_element_type=jnp.float32)
    token_grad = of_everyone(patches * token_part, "span").reshape(images, patches, D)
    return (caption_grad, token_grad)


def solution(mesh):
    torus = Mesh(
        mesh.devices.reshape(4, 8, 2, 2, mesh.shape["span"]),
        ("batch_0", "batch_1", "batch_2", "batch_3", "span"),
    )
    placed = (P(BATCH, None, None), P(BATCH_SPAN, None), P(BATCH_SPAN), P(), P(), P(), P())
    return jax.shard_map(
        on_device,
        mesh=torus,
        in_specs=placed,
        out_specs=(P(BATCH_SPAN, None), P(BATCH, None, None)),
        check_vma=False,
    )
```

profile of v0, /device:TPU:1, one launch (start us, length us, event | category | flops | bytes accessed | tf_op | source)
XLA Modules:
  0.0 529.0 jit_solution(10593747069485855426)
XLA Ops:
  1.4 22.6 %all_to_all.39 = s32[64,1,8]{2,1,0:T(1,128)S(1)} all-to-all(s32[64,1,8]{2,1,0:T(1,128)S(1)} %broadcast_in_dim.52), channel_id=1, replica_groups=mesh['batch_0'=4,'batch_1'=8,'batch_2'=2,'batch_3'=2,'span'=2] {'batch_0..., dimensions={0} | all-to-all | bytes 4096 | tf_op jit(solution)/shard_map/all_to_all | solution.py:23
  24.1 5.5 %all_to_all.40 = s32[2,1,512]{2,1,0:T(1,128)S(1)} all-to-all(s32[2,1,512]{2,1,0:T(1,128)S(1)} %reshape.92), channel_id=1, replica_groups=mesh['batch_0'=4,'batch_1'=8,'batch_2'=2,'batch_3'=2,'span'=2] {'batch_3'}, dimensions={0} | all-to-all | bytes 8192 | tf_op jit(solution)/shard_map/all_to_all | solution.py:23
  31.1 4.6 all-to-all-start
  41.5 10.6 %all-to-all-done = bf16[64,8,512]{2,1,0:T(8,128)(2,1)S(1)} async-done(((bf16[64,8,512]{2,1,0:T(8,128)(2,1)}), bf16[64,8,512]{2,1,0:T(8,128)(2,1)S(1)}, u32[]{:S(2)}, u32[]{:S(2)}) %all-to-all-start) | async-done | bytes 524320 | tf_op jit(solution)/shard_map/all_to_all | solution.py:23
  52.2 6.7 %all_to_all.41 = bf16[2,64,8,512]{3,2,1,0:T(8,128)(2,1)S(1)} all-to-all(bf16[2,64,8,512]{3,2,1,0:T(8,128)(2,1)S(1)} %broadcast_in_dim.51), channel_id=1, replica_groups=mesh['batch_0'=4,'batch_1'=8,'batch_2'=2,'batch_3'=2,'span'=2] {'batch_3'}, dimensions={0} | all-to-all | bytes 2097152 | tf_op jit(solution)/shard_map/all_to_all | solution.py:23
  60.1 390.1 %while.16 = (s32[]{:T(128)}, f32[2,256,512]{1,2,0:T(8,128)}, f32[2,256,512]{1,2,0:T(8,128)}, f32[16,1,64,512]{3,2,1,0:T(8,128)}, bf16[16,64,512]{2,1,0:T(8,128)(...) while((s32[]{:T(128)}, f32[2,256,512]{1,2,0:T(8,128)}, ...), condition=%wide.wide.region_9.10_spmd.clone, body=%wide.wide.region_0.9_spmd.clone.sunk | while | flops 412422400 | bytes 52974328 | solution.py:115
  82.6 1.8 fusion.136
  106.9 1.9 fusion.136
  124.4 1.7 fusion.133
  131.3 1.9 fusion.136
  155.7 1.9 fusion.136
  180.1 1.9 fusion.136
  204.5 1.8 fusion.136
  228.9 1.9 fusion.136
  253.2 1.9 fusion.136
  277.6 1.9 fusion.136
  302.0 1.9 fusion.136
  319.5 1.7 fusion.133
  326.4 1.9 fusion.136
  350.8 1.9 fusion.136
  375.1 1.9 fusion.136
  392.6 1.7 fusion.133
  399.5 1.9 fusion.136
  423.9 1.8 fusion.136
  448.3 1.9 fusion.136
  450.1 3.1 copy.121
  453.2 5.3 %all-to-all-start.4 = ((f32[2,64,1,8,512]{4,3,1,2,0:T(8,128)}), f32[2,64,1,8,512]{4,3,1,2,0:T(8,128)}, u32[]{:S(2)}, u32[]{:S(2)}) async-start(f32[2,64,1,8,512]{4,3,1,2,0:T(8,128)} %copy.121), calls=%async_computation.4 | async-start | bytes 4194304 | tf_op jit(solution)/shard_map/all_to_all | solution.py:45
  464.4 3.8 all-to-all-start.6
  468.1 2.9 reduce_sum.104
  471.0 23.3 %all-to-all-done.6 = f32[2,512,512]{2,1,0:T(8,128)S(1)} async-done(((f32[2,512,512]{2,1,0:T(8,128)}), f32[2,512,512]{2,1,0:T(8,128)S(1)}, u32[]{:S(2)}, u32[]{:S(2)}) %all-to-all-start.6) | async-done | bytes 2097184 | tf_op jit(solution)/shard_map/all_to_all | solution.py:23
  494.3 6.1 %all-to-all-start.5 = ((f32[64,1,8,512]{3,2,1,0:T(8,128)}), f32[64,1,8,512]{3,2,1,0:T(8,128)}, u32[]{:S(2)}, u32[]{:S(2)}) async-start(f32[64,1,8,512]{3,2,1,0:T(8,128)} %bitcast.238), calls=%async_computation.5 | async-start | bytes 2097152 | tf_op jit(solution)/shard_map/all_to_all | solution.py:52
  501.6 25.4 %all-to-all-done.5 = f32[64,1,8,512]{3,2,1,0:T(8,128)} async-done(((f32[64,1,8,512]{3,2,1,0:T(8,128)}), f32[64,1,8,512]{3,2,1,0:T(8,128)}, u32[]{:S(2)}, u32[]{:S(2)}) %all-to-all-start.5) | async-done | bytes 1048608 | tf_op jit(solution)/shard_map/all_to_all | solution.py:52
  (958 shorter events, 369.5 us)
Async XLA Ops:
  0.6 35.2 %copy-start = (bf16[2,256,512]{2,1,0:T(8,128)(2,1)S(1)}, bf16[2,256,512]{2,1,0:T(8,128)(2,1)}, u32[]{:S(2)}) copy-start(bf16[2,256,512]{2,1,0:T(8,128)(2,1)} %param.9) | copy-start | bytes 1572868
  31.1 21.0 %all-to-all-start = ((bf16[64,8,512]{2,1,0:T(8,128)(2,1)}), bf16[64,8,512]{2,1,0:T(8,128)(2,1)S(1)}, u32[]{:S(2)}, u32[]{:S(2)}) async-start(bf16[64,8,512]{2,1,0:T(8,128)(2,1)} %broadcast_in_dim.50), calls=%async_computation | async-start | bytes 1048576 | tf_op jit(solution)/shard_map/all_to_all | solution.py:23
  35.8 2.8 copy-start.13
  39.2 12.9 %copy-start.16 = (bf16[512,512]{0,1:T(8,128)(2,1)}, bf16[512,512]{0,1:T(8,128)(2,1)S(1)}, u32[]{:S(2)}) copy-start(bf16[512,512]{0,1:T(8,128)(2,1)S(1)} %copy.119) | copy-start | bytes 1572868
  52.2 7.9 %copy-start.1 = (bf16[512,512]{1,0:T(8,128)(2,1)S(1)}, bf16[512,512]{1,0:T(8,128)(2,1)}, u32[]{:S(2)}) copy-start(bf16[512,512]{1,0:T(8,128)(2,1)} %param.12) | copy-start | bytes 1572868
  52.2 7.9 %copy-start.2 = (bf16[512,512]{1,0:T(8,128)(2,1)S(1)}, bf16[512,512]{1,0:T(8,128)(2,1)}, u32[]{:S(2)}) copy-start(bf16[512,512]{1,0:T(8,128)(2,1)} %param.15) | copy-start | bytes 1572868
  60.1 6.4 %copy-start.9 = (bf16[2,256,8,64]{1,0,3,2:T(2,128)(2,1)}, bf16[2,256,8,64]{1,0,3,2:T(2,128)(2,1)S(1)}, u32[]{:S(2)}) copy-start(bf16[2,256,8,64]{1,0,3,2:T(2,128)(2,1)S(1)} %get-tuple-element.396) | copy-start | bytes 1572868 | tf_op jit(solution)/shard_map/while
  84.4 6.4 %copy-start.9 = (bf16[2,256,8,64]{1,0,3,2:T(2,128)(2,1)}, bf16[2,256,8,64]{1,0,3,2:T(2,128)(2,1)S(1)}, u32[]{:S(2)}) copy-start(bf16[2,256,8,64]{1,0,3,2:T(2,128)(2,1)S(1)} %get-tuple-element.396) | copy-start | bytes 1572868 | tf_op jit(solution)/shard_map/while
  108.8 6.4 %copy-start.9 = (bf16[2,256,8,64]{1,0,3,2:T(2,128)(2,1)}, bf16[2,256,8,64]{1,0,3,2:T(2,128)(2,1)S(1)}, u32[]{:S(2)}) copy-start(bf16[2,256,8,64]{1,0,3,2:T(2,128)(2,1)S(1)} %get-tuple-element.396) | copy-start | bytes 1572868 | tf_op jit(solution)/shard_map/while
  113.4 2.8 copy-start.11
  133.2 6.4 %copy-start.9 = (bf16[2,256,8,64]{1,0,3,2:T(2,128)(2,1)}, bf16[2,256,8,64]{1,0,3,2:T(2,128)(2,1)S(1)}, u32[]{:S(2)}) copy-start(bf16[2,256,8,64]{1,0,3,2:T(2,128)(2,1)S(1)} %get-tuple-element.396) | copy-start | bytes 1572868 | tf_op jit(solution)/shard_map/while
  157.6 6.4 %copy-start.9 = (bf16[2,256,8,64]{1,0,3,2:T(2,128)(2,1)}, bf16[2,256,8,64]{1,0,3,2:T(2,128)(2,1)S(1)}, u32[]{:S(2)}) copy-start(bf16[2,256,8,64]{1,0,3,2:T(2,128)(2,1)S(1)} %get-tuple-element.396) | copy-start | bytes 1572868 | tf_op jit(solution)/shard_map/while
  162.2 2.8 copy-start.11
  182.0 6.4 %copy-start.9 = (bf16[2,256,8,64]{1,0,3,2:T(2,128)(2,1)}, bf16[2,256,8,64]{1,0,3,2:T(2,128)(2,1)S(1)}, u32[]{:S(2)}) copy-start(bf16[2,256,8,64]{1,0,3,2:T(2,128)(2,1)S(1)} %get-tuple-element.396) | copy-start | bytes 1572868 | tf_op jit(solution)/shard_map/while
  186.6 2.8 copy-start.11
  206.3 6.4 %copy-start.9 = (bf16[2,256,8,64]{1,0,3,2:T(2,128)(2,1)}, bf16[2,256,8,64]{1,0,3,2:T(2,128)(2,1)S(1)}, u32[]{:S(2)}) copy-start(bf16[2,256,8,64]{1,0,3,2:T(2,128)(2,1)S(1)} %get-tuple-element.396) | copy-start | bytes 1572868 | tf_op jit(solution)/shard_map/while
  230.7 6.4 %copy-start.9 = (bf16[2,256,8,64]{1,0,3,2:T(2,128)(2,1)}, bf16[2,256,8,64]{1,0,3,2:T(2,128)(2,1)S(1)}, u32[]{:S(2)}) copy-start(bf16[2,256,8,64]{1,0,3,2:T(2,128)(2,1)S(1)} %get-tuple-element.396) | copy-start | bytes 1572868 | tf_op jit(solution)/shard_map/while
  255.1 6.4 %copy-start.9 = (bf16[2,256,8,64]{1,0,3,2:T(2,128)(2,1)}, bf16[2,256,8,64]{1,0,3,2:T(2,128)(2,1)S(1)}, u32[]{:S(2)}) copy-start(bf16[2,256,8,64]{1,0,3,2:T(2,128)(2,1)S(1)} %get-tuple-element.396) | copy-start | bytes 1572868 | tf_op jit(solution)/shard_map/while
  279.5 6.4 %copy-start.9 = (bf16[2,256,8,64]{1,0,3,2:T(2,128)(2,1)}, bf16[2,256,8,64]{1,0,3,2:T(2,128)(2,1)S(1)}, u32[]{:S(2)}) copy-start(bf16[2,256,8,64]{1,0,3,2:T(2,128)(2,1)S(1)} %get-tuple-element.396) | copy-start | bytes 1572868 | tf_op jit(solution)/shard_map/while
  303.9 6.4 %copy-start.9 = (bf16[2,256,8,64]{1,0,3,2:T(2,128)(2,1)}, bf16[2,256,8,64]{1,0,3,2:T(2,128)(2,1)S(1)}, u32[]{:S(2)}) copy-start(bf16[2,256,8,64]{1,0,3,2:T(2,128)(2,1)S(1)} %get-tuple-element.396) | copy-start | bytes 1572868 | tf_op jit(solution)/shard_map/while
  308.5 2.8 copy-start.11
  328.2 6.4 %copy-start.9 = (bf16[2,256,8,64]{1,0,3,2:T(2,128)(2,1)}, bf16[2,256,8,64]{1,0,3,2:T(2,128)(2,1)S(1)}, u32[]{:S(2)}) copy-start(bf16[2,256,8,64]{1,0,3,2:T(2,128)(2,1)S(1)} %get-tuple-element.396) | copy-start | bytes 1572868 | tf_op jit(solution)/shard_map/while
  352.6 6.4 %copy-start.9 = (bf16[2,256,8,64]{1,0,3,2:T(2,128)(2,1)}, bf16[2,256,8,64]{1,0,3,2:T(2,128)(2,1)S(1)}, u32[]{:S(2)}) copy-start(bf16[2,256,8,64]{1,0,3,2:T(2,128)(2,1)S(1)} %get-tuple-element.396) | copy-start | bytes 1572868 | tf_op jit(solution)/shard_map/while
  377.0 6.4 %copy-start.9 = (bf16[2,256,8,64]{1,0,3,2:T(2,128)(2,1)}, bf16[2,256,8,64]{1,0,3,2:T(2,128)(2,1)S(1)}, u32[]{:S(2)}) copy-start(bf16[2,256,8,64]{1,0,3,2:T(2,128)(2,1)S(1)} %get-tuple-element.396) | copy-start | bytes 1572868 | tf_op jit(solution)/shard_map/while
  381.6 2.8 copy-start.11
  401.4 6.4 %copy-start.9 = (bf16[2,256,8,64]{1,0,3,2:T(2,128)(2,1)}, bf16[2,256,8,64]{1,0,3,2:T(2,128)(2,1)S(1)}, u32[]{:S(2)}) copy-start(bf16[2,256,8,64]{1,0,3,2:T(2,128)(2,1)S(1)} %get-tuple-element.396) | copy-start | bytes 1572868 | tf_op jit(solution)/shard_map/while
  425.8 6.4 %copy-start.9 = (bf16[2,256,8,64]{1,0,3,2:T(2,128)(2,1)}, bf16[2,256,8,64]{1,0,3,2:T(2,128)(2,1)S(1)}, u32[]{:S(2)}) copy-start(bf16[2,256,8,64]{1,0,3,2:T(2,128)(2,1)S(1)} %get-tuple-element.396) | copy-start | bytes 1572868 | tf_op jit(solution)/shard_map/while
  453.2 5.3 %copy-start.8 = (f32[2,256,512]{1,2,0:T(8,128)S(1)}, f32[2,256,512]{1,2,0:T(8,128)}, u32[]{:S(2)}) copy-start(f32[2,256,512]{1,2,0:T(8,128)} %get-tuple-element.62) | copy-start | bytes 3145732
  453.2 6.3 %copy-start.14 = (bf16[512,512]{1,0:T(8,128)(2,1)S(1)}, bf16[512,512]{1,0:T(8,128)(2,1)}, u32[]{:S(2)}) copy-start(bf16[512,512]{1,0:T(8,128)(2,1)} %param.13) | copy-start | bytes 1572868
  453.2 9.6 %all-to-all-start.4 = ((f32[2,64,1,8,512]{4,3,1,2,0:T(8,128)}), f32[2,64,1,8,512]{4,3,1,2,0:T(8,128)}, u32[]{:S(2)}, u32[]{:S(2)}) async-start(f32[2,64,1,8,512]{4,3,1,2,0:T(8,128)} %copy.121), calls=%async_computation.4 | async-start | bytes 4194304 | tf_op jit(solution)/shard_map/all_to_all | solution.py:45
  464.4 29.9 %all-to-all-start.6 = ((f32[2,512,512]{2,1,0:T(8,128)}), f32[2,512,512]{2,1,0:T(8,128)S(1)}, u32[]{:S(2)}, u32[]{:S(2)}) async-start(f32[2,512,512]{2,1,0:T(8,128)} %broadcast_in_dim.54), calls=%async_computation.6 | async-start | bytes 4194304 | tf_op jit(solution)/shard_map/all_to_all | solution.py:23
  494.3 32.8 %all-to-all-start.5 = ((f32[64,1,8,512]{3,2,1,0:T(8,128)}), f32[64,1,8,512]{3,2,1,0:T(8,128)}, u32[]{:S(2)}, u32[]{:S(2)}) async-start(f32[64,1,8,512]{3,2,1,0:T(8,128)} %bitcast.238), calls=%async_computation.5 | async-start | bytes 2097152 | tf_op jit(solution)/shard_map/all_to_all | solution.py:52
  (157 other events, 264.8 us)
where the time goes:
time: 537 us; the launch traced here: 529 us
  matrix products  144 us (27%)
  local copies, waits for them, and re-layouts  139 us (26%)
  other arithmetic  128 us (24%)
  waiting for transfers between devices  59.3 us (11%)
  blocking collectives  34.8 us (6%)
  starting transfers between devices  19.8 us (4%)
    while x352, local copies, waits for them, and re-layouts  43.8 us
    dot_general x48, matrix products, pair_loss(): jnp.einsum('cihp,iphe->cihe', weights, value_heads, preferred_element_typ...  36.7 us
    all_to_all x3, blocking collectives, copy_for_each(): return lax.all_to_all(copies, axis, split_axis=0, concat_axis=0, tiled=True)  34.8 us
    all_to_all x2, waiting for transfers between devices, copy_for_each(): return lax.all_to_all(copies, axis, split_axis=0, concat_axis=0, tiled=True)  33.9 us
    reshape x32, local copies, waits for them, and re-layouts, pair_loss(): pooled = pooled.reshape(count * images, width).astype(jnp.bfloat16)  33.8 us
    dot_general x48, matrix products, pair_loss(): jnp.einsum('che,iphe->cihp', query_heads, key_heads, preferred_element_ty...  31.3 us
    dot_general x16, matrix products, step(): jnp.dot(grad_query, w_query.T, preferred_element_type=jnp.float32)  29.7 us
    all_to_all x1, waiting for transfers between devices, summed_rows(): return jnp.sum(lax.all_to_all(own, far, 0, 0, tiled=True), axis=0)  25.4 us
  transfers between devices with their start and end apart: 4, of which 3 were waited for; matrix products, arithmetic and copies ran while one was open for 3% of the time, Pallas kernels for 0%

commit v1 on v0

v1 whole, which is shorter than its diff:
```python
import functools

import jax
import jax.numpy as jnp
from jax import lax
from jax.experimental import pallas as pl
from jax.experimental.pallas import tpu as pltpu
from jax.sharding import Mesh
from jax.sharding import PartitionSpec as P

HEADS = 8
D = 512
PATCHES = 256
WIDE = 640
F32 = jnp.float32
BF16 = jnp.bfloat16
BATCH = ("y", "z", "x_lo", "core")
BATCH_SPAN = ("y", "z", "x_lo", "core", "span")
FAR = ("y", "z", "x_lo")

LOGIT_SCALE = 10.0
LOGIT_BIAS = -2.0
NORM_EPS = 1e-06

NN = (((1,), (0,)), ((), ()))
NT = (((1,), (1,)), ((), ()))


def dot(a, b, dims):
    return lax.dot_general(a, b, dims, preferred_element_type=F32)


def pairs_kernel(
    base_ref, tokens_ref, captions_ref, w_query_ref, w_key_ref, w_value_ref, w_out_ref,
    caption_ref, token_ref,
    queries, grad_query, direct, keys, values, weights, grad_scores, inverse, grad_keys, grad_values,
):
    images = tokens_ref.shape[0]
    low = lax.broadcasted_iota(jnp.int32, (1, 128), 1) < 64
    half = (low, jnp.logical_not(low))
    zero = jnp.zeros((), BF16)
    captions = captions_ref[:, :D]
    queries[...] = dot(captions, w_query_ref[...], NN).astype(BF16) * jnp.asarray(0.125, BF16)
    grad_query[...] = jnp.zeros_like(grad_query)
    direct[...] = jnp.zeros_like(direct)

    def of_head(h):
        return slice(h * PATCHES, (h + 1) * PATCHES)

    def of_pair(p):
        return slice(2 * p * PATCHES, (2 * p + 2) * PATCHES)

    def lanes(p):
        return slice(p * 128, (p + 1) * 128)

    def image(i, _):
        tokens = tokens_ref[i]
        k = dot(tokens, w_key_ref[...], NN).astype(BF16)
        v = dot(tokens, w_value_ref[...], NN).astype(BF16)
        for h in range(HEADS):
            keys[of_head(h), :] = jnp.where(half[h % 2], k[:, lanes(h // 2)], zero)
            values[of_head(h), :] = jnp.where(half[h % 2], v[:, lanes(h // 2)], zero)
        q = queries[...]
        pooled = []
        for p in range(HEADS // 2):
            scale = []
            for h in (2 * p, 2 * p + 1):
                scores = dot(q[:, lanes(p)], keys[of_head(h), :], NT)
                e = jnp.exp(scores - jnp.max(scores, axis=1, keepdims=True))
                weights[:, of_head(h)] = e.astype(BF16)
                scale.append(1.0 / jnp.sum(e, axis=1, keepdims=True))
            inv = jnp.where(low, scale[0], scale[1])
            inverse[:, lanes(p)] = inv
            pooled.append(dot(weights[:, of_pair(p)], values[of_pair(p), :], NN) * inv)
        pooled = jnp.concatenate(pooled, axis=1)
        mixed = dot(pooled.astype(BF16), w_out_ref[...], NN)
        caption = captions_ref[:, :D].astype(F32)
        inner = jnp.sum(mixed * caption, axis=1, keepdims=True)
        mixed_inv = lax.rsqrt(jnp.sum(mixed * mixed, axis=1, keepdims=True) + NORM_EPS)
        caption_inv = lax.rsqrt(jnp.sum(caption * caption, axis=1, keepdims=True) + NORM_EPS)
        cosine = inner * mixed_inv * caption_inv
        owner = captions_ref[:, D:].astype(F32)[:, 0:1]
        label = jnp.where(owner == (base_ref[0] + i).astype(F32), 1.0, -1.0)
        logit = LOGIT_SCALE * cosine + LOGIT_BIAS
        g = -LOGIT_SCALE * label / (1.0 + jnp.exp(label * logit))
        across = g * mixed_inv * caption_inv
        grad_mixed = across * caption - (g * cosine * mixed_inv * mixed_inv) * mixed
        direct[...] += across * mixed - (g * cosine * caption_inv * caption_inv) * caption
        grad_pooled = dot(grad_mixed.astype(BF16), w_out_ref[...], NT) * inverse[...]
        product = grad_pooled * pooled
        grad_pooled = grad_pooled.astype(BF16)
        more = []
        for p in range(HEADS // 2):
            for h in (2 * p, 2 * p + 1):
                mean = jnp.sum(jnp.where(half[h % 2], product[:, lanes(p)], 0.0), axis=1, keepdims=True)
                grad_weights = dot(grad_pooled[:, lanes(p)], values[of_head(h), :], NT)
                grad_scores[:, of_head(h)] = (
                    weights[:, of_head(h)].astype(F32) * (grad_weights - mean)
                ).astype(BF16)
            more.append(dot(grad_scores[:, of_pair(p)], keys[of_pair(p), :], NN))
        grad_query[...] += jnp.concatenate(more, axis=1)
        grad_pooled_t = grad_pooled.T
        q_t = q.T
        for h in range(HEADS):
            rows = slice(h * 64, (h + 1) * 64)
            grad_values[rows, :] = dot(grad_pooled_t[rows, :], weights[:, of_head(h)], NN)
            grad_keys[rows, :] = dot(q_t[rows, :], grad_scores[:, of_head(h)], NN)
        token_ref[i] = (
            dot(grad_keys[...].astype(BF16).T, w_key_ref[...], NT)
            + dot(grad_values[...].astype(BF16).T, w_value_ref[...], NT)
        ).astype(token_ref.dtype)
        return 0

    lax.fori_loop(0, images, image, 0)
    caption_ref[...] = (
        direct[...] + dot((grad_query[...] * 0.125).astype(BF16), w_query_ref[...], NT)
    ).astype(caption_ref.dtype)


def pairs(base, tokens, captions, w_query, w_key, w_value, w_out):
    images, count = (tokens.shape[0], captions.shape[0])
    vmem = pl.BlockSpec(memory_space=pltpu.VMEM)
    return pl.pallas_call(
        pairs_kernel,
        out_shape=(
            jax.ShapeDtypeStruct((count, D), BF16),
            jax.ShapeDtypeStruct((images, PATCHES, D), BF16),
        ),
        in_specs=[pl.BlockSpec(memory_space=pltpu.SMEM)] + [vmem] * 6,
        out_specs=(vmem, vmem),
        scratch_shapes=[
            pltpu.VMEM((count, D), BF16),
            pltpu.VMEM((count, D), F32),
            pltpu.VMEM((count, D), F32),
            pltpu.VMEM((HEADS * PATCHES, 128), BF16),
            pltpu.VMEM((HEADS * PATCHES, 128), BF16),
            pltpu.VMEM((count, HEADS * PATCHES), BF16),
            pltpu.VMEM((count, HEADS * PATCHES), BF16),
            pltpu.VMEM((count, D), F32),
            pltpu.VMEM((D, PATCHES), F32),
            pltpu.VMEM((D, PATCHES), F32),
        ],
        compiler_params=pltpu.CompilerParams(vmem_limit_bytes=40 * 1024 * 1024),
        name="pairs",
    )(base, tokens, captions, w_query, w_key, w_value, w_out)


def swapped(x, axis):
    return lax.ppermute(x, axis, ((0, 1), (1, 0)))


def on_device(image_tokens, captions, owner, w_query, w_key, w_value, w_out):
    own_images = image_tokens.shape[0]
    rows = captions.shape[0]
    side = jnp.broadcast_to(owner.astype(BF16)[:, None], (rows, WIDE - D))
    packet = jnp.concatenate([captions, side], axis=1)
    peers = lax.axis_size(FAR)
    gathered = lax.all_to_all(
        jnp.broadcast_to(packet, (peers, rows, WIDE)), FAR, split_axis=0, concat_axis=0, tiled=True
    ).reshape(peers * rows, WIDE)
    core = lax.axis_index("core")
    other_tokens = swapped(image_tokens, "core")
    chip = lax.axis_index(FAR) * (2 * own_images)
    w = (w_query, w_key, w_value, w_out)
    other_base = (chip + (1 - core) * own_images).reshape(1)
    own_base = (chip + core * own_images).reshape(1)
    caption_other, token_other = pairs(other_base, other_tokens, gathered, *w)
    caption_own, token_own = pairs(own_base, image_tokens, gathered, *w)
    token = token_own.astype(F32) + swapped(token_other, "core").astype(F32)
    token = token + swapped(token.astype(BF16), "span").astype(F32)
    token_grad = PATCHES * token
    caption = (caption_other.astype(F32) + caption_own.astype(F32)).astype(BF16)
    arrived = lax.all_to_all(
        caption.reshape(peers, rows, D), FAR, split_axis=0, concat_axis=0, tiled=True
    )
    caption_grad = 16.0 * jnp.sum(arrived.astype(F32), axis=0)
    return (caption_grad, token_grad)


def solution(mesh):
    torus = Mesh(
        mesh.devices.reshape(4, 8, 2, 2, mesh.shape["span"]),
        BATCH_SPAN,
    )
    placed = (P(BATCH, None, None), P(BATCH_SPAN, None), P(BATCH_SPAN), P(), P(), P(), P())
    return jax.shard_map(
        on_device,
        mesh=torus,
        in_specs=placed,
        out_specs=(P(BATCH_SPAN, None), P(BATCH, None, None)),
        check_vma=False,
    )
```

time: 537 us -> 92.9 us (0.17); the launches traced: 529 us -> 92.5 us
  matrix products: 144 us -> 0 us
  local copies, waits for them, and re-layouts: 139 us -> 3.84 us
  other arithmetic: 128 us -> 4.33 us
  blocking collectives: 34.8 us -> 0 us
  waiting for transfers between devices: 59.3 us -> 34.4 us
  Pallas kernels: 0 us -> 22.6 us
  starting transfers between devices: 19.8 us -> 26.7 us
    dot_general x164 -> x0, matrix products: 144 us -> none  [the longest x48 36.7 us: pair_loss(): jnp.einsum('cihp,iphe->cihe', weights, value_heads, preferred_element_typ...]
    while x354 -> x0, local copies, waits for them, and re-layouts: 45 us -> none
    reshape x96 -> x0, local copies, waits for them, and re-layouts: 41.6 us -> none  [the longest x32 33.8 us: pair_loss(): pooled = pooled.reshape(count * images, width).astype(jnp.bfloat16)]
    reduce_sum x67 -> x1, other arithmetic: 41.1 us -> 0.1 us  [on_device(): caption_grad = 16.0 * jnp.sum(arrived.astype(F32), axis=0)]
    all_to_all x3 -> x0, blocking collectives: 34.8 us -> none  [copy_for_each(): return lax.all_to_all(copies, axis, split_axis=0, concat_axis=0, tiled=True)]
    all_to_all x4 -> x2, waiting for transfers between devices: 59.3 us -> 26.9 us  [the longest x1 17.2 us: on_device(): lax.all_to_all(jnp.broadcast_to(packet, (peers, rows, WIDE)), FAR, split_...]
    mul x33 -> x2, other arithmetic: 29.4 us -> 1.81 us  [the longest x1 1.2 us: on_device(): token_grad = PATCHES * token]
    pallas_call x0 -> x2, Pallas kernels: none -> 22.6 us  [pairs(): pl.pallas_call(pairs_kernel, out_shape=(jax.ShapeDtypeStruct((count, D),...]
  transfers between devices with their start and end apart: 4 -> 5, of which waited for: 3 -> 4; matrix products, arithmetic and copies ran while one was open for 3% -> 1% of each run, Pallas kernels for 0% -> 12%
where the time goes in v1:
time: 92.9 us; the launch traced here: 92.5 us
  waiting for transfers between devices  34.4 us (37%)
  starting transfers between devices  26.7 us (29%)
  Pallas kernels  22.6 us (24%)
  other arithmetic  4.33 us (5%)
  local copies, waits for them, and re-layouts  3.84 us (4%)
    pallas_call x2, Pallas kernels, pairs(): pl.pallas_call(pairs_kernel, out_shape=(jax.ShapeDtypeStruct((count, D),...  22.6 us
    all_to_all x1, waiting for transfers between devices, on_device(): lax.all_to_all(jnp.broadcast_to(packet, (peers, rows, WIDE)), FAR, split_...  17.2 us
    all_to_all x1, starting transfers between devices, on_device(): lax.all_to_all(jnp.broadcast_to(packet, (peers, rows, WIDE)), FAR, split_...  13.7 us
    all_to_all x1, waiting for transfers between devices, on_device(): lax.all_to_all(caption.reshape(peers, rows, D), FAR, split_axis=0, concat...  9.67 us
    all_to_all x1, starting transfers between devices, on_device(): lax.all_to_all(caption.reshape(peers, rows, D), FAR, split_axis=0, concat...  7.87 us
    ppermute x3, waiting for transfers between devices, swapped(): return lax.ppermute(x, axis, ((0, 1), (1, 0)))  7.47 us
    ppermute x3, starting transfers between devices, swapped(): return lax.ppermute(x, axis, ((0, 1), (1, 0)))  5.08 us
    unnamed x14, local copies, waits for them, and re-layouts  2.88 us
  transfers between devices with their start and end apart: 5, of which 4 were waited for; matrix products, arithmetic and copies ran while one was open for 1% of the time, Pallas kernels for 12%

profile of v1, /device:TPU:1, one launch (start us, length us, event | category | flops | bytes accessed | tf_op | source)
XLA Modules:
  0.0 92.5 jit_solution(2628018332275011914)
XLA Ops:
  0.6 0.7 convert_element_type.27
  1.3 0.1 broadcast_in_dim.4
  1.4 0.7 pad_maximum_fusion
  2.1 0.0 copy-start.2
  2.1 0.9 broadcast_in_dim.10
  3.0 0.0 copy-start
  3.0 13.7 %all-to-all-start = ((bf16[64,8,640]{2,1,0:T(8,128)(2,1)}), bf16[64,8,640]{2,1,0:T(8,128)(2,1)S(1)}, u32[]{:S(2)}, u32[]{:S(2)}) async-start(bf16[64,8,640]{2,1,0:T(8,128)(2,1)} %broadcast_in_dim.10), calls=%async_computation | async-start | bytes 1310720 | tf_op jit(solution)/shard_map/all_to_all | solution.py:158
  16.7 1.0 %collective-permute-start = (bf16[2,256,512]{2,1,0:T(8,128)(2,1)}, bf16[2,256,512]{2,1,0:T(8,128)(2,1)S(1)}, u32[]{:S(2)}, u32[]{:S(2)}) collective-permute-start(bf16[2,256,512]{2,1,0:T(8,128)(2,1)} %tokens_ref.1), channel_id=1, source_target_pairs={{0,2},{2,0},{1,3},{3,1},{4,6},{6,4},{5,7},{7,5},{8,10},{10,8},{9,1... | collective-permute-start | bytes 1572872 | tf_op jit(solution)/shard_map/ppermute | solution.py:149
  17.7 17.2 %all-to-all-done = bf16[64,8,640]{2,1,0:T(8,128)(2,1)S(1)} async-done(((bf16[64,8,640]{2,1,0:T(8,128)(2,1)}), bf16[64,8,640]{2,1,0:T(8,128)(2,1)S(1)}, u32[]{:S(2)}, u32[]{:S(2)}) %all-to-all-start) | async-done | bytes 655392 | tf_op jit(solution)/shard_map/all_to_all | solution.py:158
  34.9 0.0 copy-done.2
  34.9 0.0 copy-done
  34.9 0.0 copy-done.1
  34.9 0.0 copy-start.3
  35.0 1.0 %copy-done.3 = bf16[512,512]{1,0:T(8,128)(2,1)S(1)} copy-done((bf16[512,512]{1,0:T(8,128)(2,1)S(1)}, bf16[512,512]{1,0:T(8,128)(2,1)}, u32[]{:S(2)}) %copy-start.3) | copy-done | bytes 524312
  36.0 1.0 %copy-done.4 = bf16[2,256,512]{2,1,0:T(8,128)(2,1)S(1)} copy-done((bf16[2,256,512]{2,1,0:T(8,128)(2,1)S(1)}, bf16[2,256,512]{2,1,0:T(8,128)(2,1)}, u32[]{:S(2)}) %copy-start.4) | copy-done | bytes 524312
  37.0 11.3 %pairs.3 = (bf16[512,512]{1,0:T(8,128)(2,1)S(1)}, bf16[2,256,512]{2,1,0:T(8,128)(2,1)S(1)}) custom-call(s32[1]{0:T(128)} %bitcast.2.base_ref, bf16[2,256,512]{2,1,0:T(8,128)(2,1)S(1)} %copy-done.4, bf16[512,640]{1,0:T(8,128)(2,1)S(1)} %bitcast.5, bf16[512,512]{1,0:T(8,128)(2,1)S(1)} %copy-done, bf16[512,512]{1,0:T(8,128)(2,1)S(1)} %copy-done.1, ...), custom_call_target="tpu_custom_call" | custom-call | tf_op jit(solution)/shard_map/pairs/pallas_call | solution.py:123
  48.4 0.0 collective-permute-done.tokens_ref
  48.4 11.3 %pairs.2 = (bf16[512,512]{1,0:T(8,128)(2,1)S(1)}, bf16[2,256,512]{2,1,0:T(8,128)(2,1)S(1)}) custom-call(s32[1]{0:T(128)} %bitcast.base_ref, bf16[2,256,512]{2,1,0:T(8,128)(2,1)S(1)} %collective-permute-done.tokens_ref, bf16[512,640]{1,0:T(8,128)(2,1)S(1)} %bitcast.6, bf16[512,512]{1,0:T(8,128)(2,1)S(1)} %copy-done, bf16[512,512]{1,0:T(8,128)(2,1)S(1)} %copy-done.1, ...), custom_call_target="tpu_custom_call" | custom-call | tf_op jit(solution)/shard_map/pairs/pallas_call | solution.py:123
  59.7 0.0 copy-start.5
  59.7 0.8 copy-done.5
  60.5 0.9 %fusion.1 = bf16[64,8,512]{2,1,0:T(8,128)(2,1)} fusion(bf16[512,512]{1,0:T(8,128)(2,1)S(1)} %get-tuple-element.7, bf16[512,512]{1,0:T(8,128)(2,1)S(1)} %get-tuple-element.6), kind=kLoop, calls=%fused_computation.5 | loop fusion | flops 1048576 | bytes 1572864 | tf_op jit(solution)/shard_map/reshape | solution.py:174
  61.4 7.9 %all-to-all-start.1 = ((bf16[64,8,512]{2,1,0:T(8,128)(2,1)}), bf16[64,8,512]{2,1,0:T(8,128)(2,1)S(1)}, u32[]{:S(2)}, u32[]{:S(2)}) async-start(bf16[64,8,512]{2,1,0:T(8,128)(2,1)} %fusion.1), calls=%async_computation.1 | async-start | bytes 1048576 | tf_op jit(solution)/shard_map/all_to_all | solution.py:173
  69.3 0.0 copy-done.6
  69.3 1.5 %collective-permute-start.1 = (bf16[2,256,512]{2,1,0:T(8,128)(2,1)S(1)}, bf16[2,256,512]{2,1,0:T(8,128)(2,1)S(1)}, u32[]{:S(2)}, u32[]{:S(2)}) collective-permute-start(bf16[2,256,512]{2,1,0:T(8,128)(2,1)S(1)} %copy-done.6), channel_id=1, source_target_pairs={{0,2},{2,0},{1,3},{3,1},{4,6},{6,4},{5,7},{7,5},{8,10},{10,8},{9,1... | collective-permute-start | bytes 1572872 | tf_op jit(solution)/shard_map/ppermute | solution.py:149
  70.8 1.5 %collective-permute-done.1 = bf16[2,256,512]{2,1,0:T(8,128)(2,1)S(1)} collective-permute-done((bf16[2,256,512]{2,1,0:T(8,128)(2,1)S(1)}, bf16[2,256,512]{2,1,0:T(8,128)(2,1)S(1)}, u32[]{:S(2)}, u32[]{:S(2)}) %collective-permute-start.1) | collective-permute-done | bytes 524320 | tf_op jit(solution)/shard_map/ppermute | solution.py:149
  72.3 0.1 fusion
  72.5 2.5 %collective-permute-start.2 = (bf16[2,256,512]{2,1,0:T(8,128)(2,1)S(1)}, bf16[2,256,512]{2,1,0:T(8,128)(2,1)S(1)}, u32[]{:S(2)}, u32[]{:S(2)}) collective-permute-start(bf16[2,256,512]{2,1,0:T(8,128)(2,1)S(1)} %fusion), channel_id=1, source_target_pairs={{0,1},{1,0},{2,3},{3,2},{4,5},{5,4},{6,7},{7,6},{8,9},{9,8},{10,11... | collective-permute-start | bytes 1572872 | tf_op jit(solution)/shard_map/ppermute | solution.py:149
  75.0 9.7 %all-to-all-done.1 = bf16[64,8,512]{2,1,0:T(8,128)(2,1)S(1)} async-done(((bf16[64,8,512]{2,1,0:T(8,128)(2,1)}), bf16[64,8,512]{2,1,0:T(8,128)(2,1)S(1)}, u32[]{:S(2)}, u32[]{:S(2)}) %all-to-all-start.1) | async-done | bytes 524320 | tf_op jit(solution)/shard_map/all_to_all | solution.py:173
  84.7 0.1 convert_reduce_fusion
  84.8 0.6 broadcast_multiply_fusion
  85.4 5.9 %collective-permute-done.2 = bf16[2,256,512]{2,1,0:T(8,128)(2,1)S(1)} collective-permute-done((bf16[2,256,512]{2,1,0:T(8,128)(2,1)S(1)}, bf16[2,256,512]{2,1,0:T(8,128)(2,1)S(1)}, u32[]{:S(2)}, u32[]{:S(2)}) %collective-permute-start.2) | collective-permute-done | bytes 524320 | tf_op jit(solution)/shard_map/ppermute | solution.py:149
  91.3 1.2 %add_multiply_fusion = f32[2,256,512]{2,1,0:T(8,128)} fusion(bf16[2,256,512]{2,1,0:T(8,128)(2,1)S(1)} %collective-permute-done.2, bf16[2,256,512]{2,1,0:T(8,128)(2,1)S(1)} %collective-permute-done.1, bf16[2,256,512]{2,1,0:T(8,128)(2,1)S(1)} %get-tuple-element.8), kind=kLoop, calls=%fused_computation | loop fusion | flops 1572864 | bytes 2621440 | tf_op jit(solution)/shard_map/mul | solution.py:171
  (3 shorter events, 0.0 us)
Async XLA Ops:
  2.1 32.9 %copy-start.2 = (bf16[512,512]{1,0:T(8,128)(2,1)S(1)}, bf16[512,512]{1,0:T(8,128)(2,1)}, u32[]{:S(2)}) copy-start(bf16[512,512]{1,0:T(8,128)(2,1)} %w_value_ref.3) | copy-start | bytes 1572868
  3.0 32.0 %copy-start = (bf16[512,512]{1,0:T(8,128)(2,1)S(1)}, bf16[512,512]{1,0:T(8,128)(2,1)}, u32[]{:S(2)}) copy-start(bf16[512,512]{1,0:T(8,128)(2,1)} %w_query_ref.3) | copy-start | bytes 1572868
  3.0 32.0 %copy-start.1 = (bf16[512,512]{1,0:T(8,128)(2,1)S(1)}, bf16[512,512]{1,0:T(8,128)(2,1)}, u32[]{:S(2)}) copy-start(bf16[512,512]{1,0:T(8,128)(2,1)} %w_key_ref.3) | copy-start | bytes 1572868
  3.0 32.0 %all-to-all-start = ((bf16[64,8,640]{2,1,0:T(8,128)(2,1)}), bf16[64,8,640]{2,1,0:T(8,128)(2,1)S(1)}, u32[]{:S(2)}, u32[]{:S(2)}) async-start(bf16[64,8,640]{2,1,0:T(8,128)(2,1)} %broadcast_in_dim.10), calls=%async_computation | async-start | bytes 1310720 | tf_op jit(solution)/shard_map/all_to_all | solution.py:158
  16.7 31.7 %collective-permute-start = (bf16[2,256,512]{2,1,0:T(8,128)(2,1)}, bf16[2,256,512]{2,1,0:T(8,128)(2,1)S(1)}, u32[]{:S(2)}, u32[]{:S(2)}) collective-permute-start(bf16[2,256,512]{2,1,0:T(8,128)(2,1)} %tokens_ref.1), channel_id=1, source_target_pairs={{0,2},{2,0},{1,3},{3,1},{4,6},{6,4},{5,7},{7,5},{8,10},{10,8},{9,1... | collective-permute-start | bytes 1572872 | tf_op jit(solution)/shard_map/ppermute | solution.py:149
  34.9 1.0 %copy-start.3 = (bf16[512,512]{1,0:T(8,128)(2,1)S(1)}, bf16[512,512]{1,0:T(8,128)(2,1)}, u32[]{:S(2)}) copy-start(bf16[512,512]{1,0:T(8,128)(2,1)} %w_out_ref.3) | copy-start | bytes 1572868
  36.0 1.0 %copy-start.4 = (bf16[2,256,512]{2,1,0:T(8,128)(2,1)S(1)}, bf16[2,256,512]{2,1,0:T(8,128)(2,1)}, u32[]{:S(2)}) copy-start(bf16[2,256,512]{2,1,0:T(8,128)(2,1)} %tokens_ref.1) | copy-start | bytes 1572868
  59.7 0.8 copy-start.5
  61.4 7.9 %copy-start.6 = (bf16[2,256,512]{2,1,0:T(8,128)(2,1)S(1)}, bf16[2,256,512]{2,1,0:T(8,128)(2,1)}, u32[]{:S(2)}) copy-start(bf16[2,256,512]{2,1,0:T(8,128)(2,1)} %copy-done.5) | copy-start | bytes 1572868
  61.4 23.3 %all-to-all-start.1 = ((bf16[64,8,512]{2,1,0:T(8,128)(2,1)}), bf16[64,8,512]{2,1,0:T(8,128)(2,1)S(1)}, u32[]{:S(2)}, u32[]{:S(2)}) async-start(bf16[64,8,512]{2,1,0:T(8,128)(2,1)} %fusion.1), calls=%async_computation.1 | async-start | bytes 1048576 | tf_op jit(solution)/shard_map/all_to_all | solution.py:173
  69.3 3.0 %collective-permute-start.1 = (bf16[2,256,512]{2,1,0:T(8,128)(2,1)S(1)}, bf16[2,256,512]{2,1,0:T(8,128)(2,1)S(1)}, u32[]{:S(2)}, u32[]{:S(2)}) collective-permute-start(bf16[2,256,512]{2,1,0:T(8,128)(2,1)S(1)} %copy-done.6), channel_id=1, source_target_pairs={{0,2},{2,0},{1,3},{3,1},{4,6},{6,4},{5,7},{7,5},{8,10},{10,8},{9,1... | collective-permute-start | bytes 1572872 | tf_op jit(solution)/shard_map/ppermute | solution.py:149
  72.5 18.8 %collective-permute-start.2 = (bf16[2,256,512]{2,1,0:T(8,128)(2,1)S(1)}, bf16[2,256,512]{2,1,0:T(8,128)(2,1)S(1)}, u32[]{:S(2)}, u32[]{:S(2)}) collective-permute-start(bf16[2,256,512]{2,1,0:T(8,128)(2,1)S(1)} %fusion), channel_id=1, source_target_pairs={{0,1},{1,0},{2,3},{3,2},{4,5},{5,4},{6,7},{7,6},{8,9},{9,8},{10,11... | collective-permute-start | bytes 1572872 | tf_op jit(solution)/shard_map/ppermute | solution.py:149

commit v2 on v1

v2 whole, which is shorter than its diff:
```python
import functools

import jax
import jax.numpy as jnp
from jax import lax
from jax.experimental import pallas as pl
from jax.experimental.pallas import tpu as pltpu
from jax.sharding import Mesh
from jax.sharding import PartitionSpec as P

HEADS = 8
HEAD_DIM = 64
D = 512
PATCHES = 256
CHUNK = 256
WIDE = 640
F32 = jnp.float32
BF16 = jnp.bfloat16
BATCH = ("y", "z", "x_lo", "core")
BATCH_SPAN = ("y", "z", "x_lo", "core", "span")
FAR = ("y", "z", "x_lo")
PLANE = ("y", "z")

LOGIT_SCALE = 10.0
LOGIT_BIAS = -2.0
NORM_EPS = 1e-06
LOG2E = 1.4426950408889634

NN = (((1,), (0,)), ((), ()))
NT = (((1,), (1,)), ((), ()))


def dot(a, b, dims=NN):
    return lax.dot_general(a, b, dims, preferred_element_type=F32)


def head(h):
    return slice(h * HEAD_DIM, (h + 1) * HEAD_DIM)


def pair(h):
    return slice((h // 2) * 128, (h // 2 + 1) * 128)


def patches_of(h):
    return slice(h * PATCHES, (h + 1) * PATCHES)


def prepare_captions(packet_ref, w_query_ref, q_ref, qt_ref, cap_ref, side_ref):
    captions = packet_ref[:, :D]
    query = dot(captions, w_query_ref[...]).astype(BF16) * jnp.asarray(0.125, BF16)
    q_ref[...] = query
    qt_ref[...] = query.T
    cap_ref[...] = captions.T
    cap = cap_ref[...].astype(F32)
    norm = lax.rsqrt(jnp.sum(cap * cap, axis=0, keepdims=True) + NORM_EPS)
    owner = packet_ref[:, D:].T.astype(F32)
    side_ref[0:8, :] = owner[0:8, :]
    side_ref[8:16, :] = jnp.broadcast_to(norm, (8, CHUNK))


def fill_zeros(padded):
    zero = jnp.zeros((HEAD_DIM, CHUNK), BF16)
    for h in range(HEADS):
        high = 128 * h + 64 * (1 - h % 2)
        padded[high : high + 64, :] = zero


def prepare_image(kv, kz, va, kt, vt_ref):
    lane = lax.broadcasted_iota(jnp.int32, (1, 128), 1)
    low = lane < 64
    zero = jnp.zeros((), BF16)
    kt[...] = kv[:, :D].T
    vt = kv[:, D:].T
    one = jnp.ones((16, PATCHES), BF16)
    for h in range(HEADS):
        mine = low if h % 2 == 0 else jnp.logical_not(low)
        start = 64 * (1 - h % 2)
        fill = jnp.where((lane == start) | (lane == start + 1), 1.0, 0.0).astype(BF16)
        p = h // 2
        kz[patches_of(h), :] = jnp.where(mine, kv[:, 128 * p : 128 * p + 128], zero)
        va[patches_of(h), :] = jnp.where(mine, kv[:, D + 128 * p : D + 128 * p + 128], fill)
        vt_ref[80 * h : 80 * h + 64, :] = vt[head(h), :]
        vt_ref[80 * h + 64 : 80 * h + 80, :] = one


def unit(image_id, img, block, w_out_t, w_out, slot, dq, dd, dk, dv, fresh_cap, fresh_img):
    kz, va, kt, vt = img
    q, qt, cap, side = block
    es, ds, pooled_s, gz = slot
    invs = []

    def scores_of(h):
        return dot(q[:, pair(h)], kz[patches_of(h), :], NT)

    coming = scores_of(0)
    for h in range(HEADS):
        scores = coming
        if h + 1 < HEADS:
            coming = scores_of(h + 1)
        top = jnp.max(scores, axis=1, keepdims=True)
        e = jnp.exp2((scores - top) * LOG2E).astype(BF16)
        es[:, patches_of(h)] = e
        both = dot(vt[80 * h : 80 * h + 80, :], e, NT)
        inv = 1.0 / both[64:65, :]
        invs.append(inv)
        pooled_s[head(h), :] = both[0:64, :] * inv
        yield
    pooled = pooled_s[...]
    mixed = dot(w_out_t[...], pooled.astype(BF16))
    caption = cap[...].astype(F32)
    inner = jnp.sum(mixed * caption, axis=0, keepdims=True)
    mixed_inv = lax.rsqrt(jnp.sum(mixed * mixed, axis=0, keepdims=True) + NORM_EPS)
    caption_inv = side[8:9, :]
    cosine = inner * mixed_inv * caption_inv
    label = jnp.where(side[0:1, :] == image_id, 1.0, -1.0)
    logit = LOGIT_SCALE * cosine + LOGIT_BIAS
    g = -LOGIT_SCALE * label / (1.0 + jnp.exp(label * logit))
    across = g * mixed_inv * caption_inv
    grad_mixed = across * caption - (g * cosine * mixed_inv * mixed_inv) * mixed
    straight = across * mixed - (g * cosine * caption_inv * caption_inv) * caption
    if fresh_cap:
        dd[...] = straight
    else:
        dd[...] += straight
    grad_pooled = dot(w_out[...], grad_mixed.astype(BF16))
    row = lax.broadcasted_iota(jnp.int32, (16, 1), 0)
    gps = []
    for h in range(HEADS):
        gp = grad_pooled[head(h), :] * invs[h]
        mean = -jnp.sum(gp * pooled_s[head(h), :], axis=0, keepdims=True)
        gp = gp.astype(BF16)
        gps.append(gp)
        coarse = mean.astype(BF16).astype(F32)
        both = jnp.where(row == 0, coarse, jnp.where(row == 1, mean - coarse, 0.0)).astype(BF16)
        low = 128 * h + 64 * (h % 2)
        high = 128 * h + 64 * (1 - h % 2)
        gz[low : low + 64, :] = gp
        gz[high : high + 16, :] = both
    yield

    def weights_of(h):
        return dot(gz[128 * h : 128 * h + 128, :].T, va[patches_of(h), :], NT)

    coming = weights_of(0)
    for h in range(HEADS):
        gw = coming
        if h + 1 < HEADS:
            coming = weights_of(h + 1)
        e = es[:, patches_of(h)]
        gs = (e.astype(F32) * gw).astype(BF16)
        ds[:, patches_of(h)] = gs
        more = dot(kt[head(h), :], gs, NT)
        mv = dot(gps[h], e)
        mk = dot(qt[head(h), :], gs)
        if fresh_cap:
            dq[head(h), :] = more
        else:
            dq[head(h), :] += more
        if fresh_img:
            dk[head(h), :] = mk
            dv[head(h), :] = mv
        else:
            dk[head(h), :] += mk
            dv[head(h), :] += mv
        yield


def pipeline(units):
    step = HEADS + 1
    ahead = units[0]
    for _ in range(step):
        next(ahead)
    for n in range(len(units)):
        current = units[n]
        after = units[n + 1] if n + 1 < len(units) else None
        for _ in range(HEADS):
            next(current)
            if after is not None:
                next(after)
        if after is not None:
            next(after)


def slots(count=2):
    one = [
        pltpu.VMEM((CHUNK, HEADS * PATCHES), BF16),
        pltpu.VMEM((CHUNK, HEADS * PATCHES), BF16),
        pltpu.VMEM((D, CHUNK), F32),
        pltpu.VMEM((1024, CHUNK), BF16),
    ]
    return one * count


IMAGE_SCRATCH = [
    pltpu.VMEM((HEADS * PATCHES, 128), BF16),
    pltpu.VMEM((HEADS * PATCHES, 128), BF16),
    pltpu.VMEM((D, PATCHES), BF16),
    pltpu.VMEM((640, PATCHES), BF16),
]
VM = pl.BlockSpec(memory_space=pltpu.VMEM)
SM = pl.BlockSpec(memory_space=pltpu.SMEM)
PARAMS = pltpu.CompilerParams(vmem_limit_bytes=28 * 1024 * 1024)
BLOCK = (
    jax.ShapeDtypeStruct((CHUNK, D), BF16),
    jax.ShapeDtypeStruct((D, CHUNK), BF16),
    jax.ShapeDtypeStruct((D, CHUNK), BF16),
    jax.ShapeDtypeStruct((16, CHUNK), F32),
)
TOTAL = jax.ShapeDtypeStruct((D, CHUNK), F32)


def project_kernel(tokens, w_key, w_value, out):
    for i in range(2):
        out[i, :, :D] = dot(tokens[i], w_key[...]).astype(BF16)
        out[i, :, D:] = dot(tokens[i], w_value[...]).astype(BF16)


def project(tokens, w_key, w_value):
    return pl.pallas_call(
        project_kernel,
        out_shape=jax.ShapeDtypeStruct((2, PATCHES, 2 * D), BF16),
        in_specs=[VM] * 3,
        out_specs=VM,
        compiler_params=PARAMS,
        cost_estimate=pl.CostEstimate(flops=2 * 512 * 512 * 1024, bytes_accessed=2**21, transcendentals=0),
        name="project",
    )(tokens, w_key, w_value)


def images_of(kv, scratch):
    images = []
    for i in range(2):
        img = scratch[4 * i : 4 * i + 4]
        prepare_image(kv.at[i], *img)
        images.append(img)
    return images


def first_kernel(base, packet, kv, w_query, w_out_t, w_out, q, qt, cap, side, dq, dd, dkv, *s):
    block = (q, qt, cap, side)
    prepare_captions(packet, w_query, *block)
    images = images_of(kv, s[:8])
    s = s[8:]
    units = []
    for i in range(2):
        slot = s[4 * i : 4 * i + 4]
        fill_zeros(slot[3])
        units.append(
            unit(
                (base[0] + i).astype(F32), images[i], block, w_out_t, w_out, slot,
                dq, dd, dkv.at[i, 0], dkv.at[i, 1], i == 0, True,
            )
        )
    pipeline(units)


def first(base, packet, kv, w_query, w_out_t, w_out):
    return pl.pallas_call(
        first_kernel,
        out_shape=(*BLOCK, TOTAL, TOTAL, jax.ShapeDtypeStruct((2, 2, D, PATCHES), F32)),
        in_specs=[SM] + [VM] * 5,
        out_specs=(VM,) * 7,
        scratch_shapes=IMAGE_SCRATCH * 2 + slots(),
        compiler_params=PARAMS,
        cost_estimate=pl.CostEstimate(flops=2 * 10**9, bytes_accessed=2**22, transcendentals=2**20),
        name="first",
    )(base, packet, kv, w_query, w_out_t, w_out)


def second_kernel(
    base, packet, kv, w_query, w_out_t, w_out, qa, qta, capa, sidea, dqa_in, dda_in,
    q, qt, cap, side, dqa, dda, dqb, ddb, dkv_b, dk, dv, *s,
):
    block_a = (qa, qta, capa, sidea)
    block_b = (q, qt, cap, side)
    prepare_captions(packet, w_query, *block_b)
    images = images_of(kv, s[:8])
    s = s[8:]
    fill_zeros(s[3])
    fill_zeros(s[7])
    dqa[...] = dqa_in[...]
    dda[...] = dda_in[...]
    units = []
    for i in range(2):
        name = (base[0] + i).astype(F32)
        img = images[i]
        units.append(
            unit(name, img, block_a, w_out_t, w_out, s[0:4], dqa, dda, dk.at[i], dv.at[i], False, True)
        )
        units.append(
            unit(name, img, block_b, w_out_t, w_out, s[4:8], dqb, ddb, dk.at[i], dv.at[i], i == 0, False)
        )
    pipeline(units)
    for i in range(2):
        dkv_b[i, 0] = dk[i].astype(BF16)
        dkv_b[i, 1] = dv[i].astype(BF16)


def second(base, packet, kv, w_query, w_out_t, w_out, block_a, dqa, dda):
    return pl.pallas_call(
        second_kernel,
        out_shape=(*BLOCK, TOTAL, TOTAL, TOTAL, TOTAL, jax.ShapeDtypeStruct((2, 2, D, PATCHES), BF16)),
        in_specs=[SM] + [VM] * 11,
        out_specs=(VM,) * 9,
        scratch_shapes=[pltpu.VMEM((2, D, PATCHES), F32)] * 2 + IMAGE_SCRATCH * 2 + slots(),
        compiler_params=PARAMS,
        cost_estimate=pl.CostEstimate(flops=4 * 10**9, bytes_accessed=2**22, transcendentals=2**21),
        name="second",
    )(base, packet, kv, w_query, w_out_t, w_out, *block_a, dqa, dda)


def third_kernel(
    base, kv, w_query, w_key, w_value, w_out_t, w_out, q, qt, cap, side, dqa, dda, dqb_in, ddb_in, dkv_in, arrived,
    caption_out, token_out, dqb, ddb, dk, dv, *s,
):
    block = (q, qt, cap, side)
    images = images_of(kv, s[:8])
    s = s[8:]
    fill_zeros(s[3])
    fill_zeros(s[7])
    dqb[...] = dqb_in[...]
    ddb[...] = ddb_in[...]
    units = []
    for i in range(2):
        units.append(
            unit(
                (base[0] + i).astype(F32), images[i], block, w_out_t, w_out, s[4 * i : 4 * i + 4],
                dqb, ddb, dk.at[i], dv.at[i], False, True,
            )
        )
    pipeline(units)
    for i in range(2):
        gk = dkv_in[i, 0] + arrived[i, 0].astype(F32) + dk[i]
        gv = dkv_in[i, 1] + arrived[i, 1].astype(F32) + dv[i]
        token = dot(w_key[...], gk.astype(BF16)) + dot(w_value[...], gv.astype(BF16))
        token_out[i] = token.astype(BF16).T
    here = base[1]
    for where, dq, dd in ((here, dqa, dda), (1 - here, dqb, ddb)):
        total = dd[...] + dot(w_query[...], (dq[...] * 0.125).astype(BF16))
        caption_out[:, pl.ds(where, 1)] = total.astype(BF16).T.reshape(32, 1, 8, D)


def third(base, kv, w_query, w_key, w_value, w_out_t, w_out, block, dqa, dda, dqb, ddb, dkv, arrived):
    return pl.pallas_call(
        third_kernel,
        out_shape=(
            jax.ShapeDtypeStruct((32, 2, 8, D), BF16),
            jax.ShapeDtypeStruct((2, PATCHES, D), BF16),
        ),
        in_specs=[SM] + [VM] * 16,
        out_specs=(VM,) * 2,
        scratch_shapes=[pltpu.VMEM((D, CHUNK), F32)] * 2
        + [pltpu.VMEM((2, D, PATCHES), F32)] * 2
        + IMAGE_SCRATCH * 2
        + slots(),
        compiler_params=PARAMS,
        cost_estimate=pl.CostEstimate(flops=2 * 10**9, bytes_accessed=2**22, transcendentals=2**20),
        name="third",
    )(base, kv, w_query, w_key, w_value, w_out_t, w_out, *block, dqa, dda, dqb, ddb, dkv, arrived)


def swapped(x, axis):
    return lax.ppermute(x, axis, ((0, 1), (1, 0)))


def on_device(image_tokens, captions, owner, w_query, w_key, w_value, w_out):
    own_images = image_tokens.shape[0]
    rows = captions.shape[0]
    side = jnp.broadcast_to(owner.astype(BF16)[:, None], (rows, WIDE - D))
    packet = jnp.concatenate([captions, side], axis=1)
    peers = lax.axis_size(PLANE)
    near = lax.all_to_all(
        jnp.broadcast_to(packet, (peers, rows, WIDE)), PLANE, split_axis=0, concat_axis=0, tiled=True
    ).reshape(peers * rows, WIDE)
    kv_own = project(image_tokens, w_key, w_value)
    kv_other = swapped(kv_own, "core")
    far = swapped(near, "x_lo")
    w_out_t = w_out.T
    core = lax.axis_index("core")
    chip = lax.axis_index(FAR) * (2 * own_images)
    x_lo = lax.axis_index("x_lo")
    base_own = jnp.stack([chip + core * own_images, x_lo])
    base_other = jnp.stack([chip + (1 - core) * own_images, x_lo])
    *block_a, dqa, dda, dkv = first(base_own, near, kv_own, w_query, w_out_t, w_out)
    *block_b, dqa, dda, dqb, ddb, dkv_other = second(
        base_other, far, kv_other, w_query, w_out_t, w_out, block_a, dqa, dda
    )
    arrived = swapped(dkv_other, "core")
    caption, token = third(
        base_own, kv_own, w_query, w_key, w_value, w_out_t, w_out, block_b, dqa, dda, dqb, ddb, dkv, arrived
    )
    other_half = swapped(token, "span")
    token_grad = PATCHES * (token.astype(F32) + other_half.astype(F32))
    sent = lax.all_to_all(caption.reshape(2 * peers, rows, D), FAR, split_axis=0, concat_axis=0, tiled=True)
    caption_grad = 16.0 * jnp.sum(sent.astype(F32), axis=0)
    return (caption_grad, token_grad)


def solution(mesh):
    torus = Mesh(mesh.devices.reshape(4, 8, 2, 2, mesh.shape["span"]), BATCH_SPAN)
    placed = (P(BATCH, None, None), P(BATCH_SPAN, None), P(BATCH_SPAN), P(), P(), P(), P())
    return jax.shard_map(
        on_device,
        mesh=torus,
        in_specs=placed,
        out_specs=(P(BATCH_SPAN, None), P(BATCH, None, None)),
        check_vma=False,
    )
```

time: 92.9 us -> 92.4 us (level)
  blocking collectives: 0 us -> 20.3 us
  waiting for transfers between devices: 34.4 us -> 19.9 us
  starting transfers between devices: 26.7 us -> 17.9 us
  Pallas kernels: 22.6 us -> 27.9 us
  other arithmetic: 4.33 us -> 1.95 us
    all_to_all x2 -> x1, waiting for transfers between devices: 26.9 us -> 0.01 us  [on_device(): lax.all_to_all(caption.reshape(2 * peers, rows, D), FAR, split_axis=0, co...]
    all_to_all x0 -> x1, blocking collectives: none -> 20.3 us  [on_device(): lax.all_to_all(jnp.broadcast_to(packet, (peers, rows, WIDE)), PLANE, spli...]
    all_to_all x2 -> x1, starting transfers between devices: 21.6 us -> 7.69 us  [on_device(): lax.all_to_all(caption.reshape(2 * peers, rows, D), FAR, split_axis=0, co...]
    ppermute x3 -> x4, waiting for transfers between devices: 7.47 us -> 19.9 us  [swapped(): return lax.ppermute(x, axis, ((0, 1), (1, 0)))]
    pallas_call x2 -> x4, Pallas kernels: 22.6 us -> 27.9 us  [the longest x1 13 us: second(): pl.pallas_call(second_kernel, out_shape=(*BLOCK, TOTAL, TOTAL, TOTAL, TOT...]
    ppermute x3 -> x4, starting transfers between devices: 5.08 us -> 10.2 us  [swapped(): return lax.ppermute(x, axis, ((0, 1), (1, 0)))]
    reshape x1 -> x0, other arithmetic: 0.93 us -> none  [on_device(): caption.reshape(peers, rows, D)]
    unnamed x14 -> x19, local copies, waits for them, and re-layouts: 2.88 us -> 3.36 us
  transfers between devices with their start and end apart: 5 -> 5, of which waited for: 4 -> 2; matrix products, arithmetic and copies ran while one was open for 1% -> 2% of each run, Pallas kernels for 12% -> 7%
where the time goes in v2:
time: 92.4 us; the launch traced here: 92.1 us
  Pallas kernels  27.9 us (30%)
  blocking collectives  20.3 us (22%)
  waiting for transfers between devices  19.9 us (22%)
  starting transfers between devices  17.9 us (19%)
  local copies, waits for them, and re-layouts  3.46 us (4%)
  other arithmetic  1.95 us (2%)
    all_to_all x1, blocking collectives, on_device(): lax.all_to_all(jnp.broadcast_to(packet, (peers, rows, WIDE)), PLANE, spli...  20.3 us
    ppermute x4, waiting for transfers between devices, swapped(): return lax.ppermute(x, axis, ((0, 1), (1, 0)))  19.9 us
    pallas_call x1, Pallas kernels, second(): pl.pallas_call(second_kernel, out_shape=(*BLOCK, TOTAL, TOTAL, TOTAL, TOT...  13 us
    ppermute x4, starting transfers between devices, swapped(): return lax.ppermute(x, axis, ((0, 1), (1, 0)))  10.2 us
    pallas_call x1, Pallas kernels, third(): pl.pallas_call(third_kernel, out_shape=(jax.ShapeDtypeStruct((32, 2, 8, D...  7.78 us
    all_to_all x1, starting transfers between devices, on_device(): lax.all_to_all(caption.reshape(2 * peers, rows, D), FAR, split_axis=0, co...  7.69 us
    pallas_call x1, Pallas kernels, first(): pl.pallas_call(first_kernel, out_shape=(*BLOCK, TOTAL, TOTAL, jax.ShapeDt...  6.41 us
    unnamed x19, local copies, waits for them, and re-layouts  3.36 us
  transfers between devices with their start and end apart: 5, of which 2 were waited for; matrix products, arithmetic and copies ran while one was open for 2% of the time, Pallas kernels for 7%

profile of v2, /device:TPU:1, one launch (start us, length us, event | category | flops | bytes accessed | tf_op | source)
XLA Modules:
  0.0 92.1 jit_solution(13716080908304306020)
XLA Ops:
  0.6 0.0 copy-start
  0.6 1.0 %copy-done = bf16[512,512]{1,0:T(8,128)(2,1)S(1)} copy-done((bf16[512,512]{1,0:T(8,128)(2,1)S(1)}, bf16[512,512]{1,0:T(8,128)(2,1)}, u32[]{:S(2)}) %copy-start) | copy-done | bytes 524312
  1.7 1.0 %copy-done.2 = bf16[512,512]{1,0:T(8,128)(2,1)S(1)} copy-done((bf16[512,512]{1,0:T(8,128)(2,1)S(1)}, bf16[512,512]{1,0:T(8,128)(2,1)}, u32[]{:S(2)}) %copy-start.2) | copy-done | bytes 524312
  2.7 1.0 %copy-done.5 = bf16[2,256,512]{2,1,0:T(8,128)(2,1)S(1)} copy-done((bf16[2,256,512]{2,1,0:T(8,128)(2,1)S(1)}, bf16[2,256,512]{2,1,0:T(8,128)(2,1)}, u32[]{:S(2)}) %copy-start.5) | copy-done | bytes 524312
  3.8 0.7 project.1.kv
  4.5 3.3 %collective-permute-start.1 = (bf16[2,256,1024]{2,1,0:T(8,128)(2,1)S(1)}, bf16[2,256,1024]{2,1,0:T(8,128)(2,1)}, u32[]{:S(2)}, u32[]{:S(2)}) collective-permute-start(bf16[2,256,1024]{2,1,0:T(8,128)(2,1)S(1)} %project.1.kv), channel_id=1, source_target_pairs={{0,2},{2,0},{1,3},{3,1},{4,6},{6,4},{5,7},{7,5},{8,10},{10,8},{9,1... | collective-permute-start | bytes 3145736 | tf_op jit(solution)/shard_map/ppermute | solution.py:364
  7.8 0.0 copy-done.8
  7.8 0.1 broadcast_in_dim.4
  7.9 0.0 copy-done.7
  7.9 20.3 %all_to_all.10 = bf16[32,8,640]{2,1,0:T(8,128)(2,1)S(1)} all-to-all(bf16[32,8,640]{2,1,0:T(8,128)(2,1)S(1)} %broadcast_in_dim.10), channel_id=1, replica_groups=mesh['y'=4,'z'=8,'x_lo'=2,'core'=2,'span'=2] {'y','z'}, dimensions={0} | all-to-all | bytes 655360 | tf_op jit(solution)/shard_map/all_to_all | solution.py:373
  28.2 1.2 %collective-permute-start = (bf16[256,640]{1,0:T(8,128)(2,1)S(1)}, bf16[256,640]{1,0:T(8,128)(2,1)S(1)}, u32[]{:S(2)}, u32[]{:S(2)}) collective-permute-start(bf16[256,640]{1,0:T(8,128)(2,1)S(1)} %bitcast.9), channel_id=1, source_target_pairs={{0,4},{4,0},{1,5},{5,1},{2,6},{6,2},{3,7},{7,3},{8,12},{12,8},{9,1... | collective-permute-start | bytes 983048 | tf_op jit(solution)/shard_map/ppermute | solution.py:364
  29.4 0.0 copy-done.4
  29.4 0.2 copy.9
  29.6 0.1 pad_add_fusion
  29.7 0.0 copy-done.6
  29.7 6.4 %first.1 = (bf16[256,512]{1,0:T(8,128)(2,1)S(1)}, bf16[512,256]{1,0:T(8,128)(2,1)S(1)}, bf16[512,256]{1,0:T(8,128)(2,1)S(1)}, f32[16,256]{1,0:T(8,128)S(1)}, f32...) custom-call(s32[2]{0:T(128)S(1)} %get-tuple-element.38.base, ...), custom_call_target="tpu_custom_call" | custom-call | flops 2000000000 | bytes 4194304 | tf_op jit(solution)/shard_map/first/pallas_call | solution.py:259
  36.1 0.0 collective-permute-done.packet
  36.1 0.0 collective-permute-done.1.kv
  36.1 0.0 copy-start.1
  36.1 0.0 copy-start.3
  36.1 13.0 %second.1 = (bf16[256,512]{1,0:T(8,128)(2,1)S(1)}, bf16[512,256]{1,0:T(8,128)(2,1)S(1)}, bf16[512,256]{1,0:T(8,128)(2,1)S(1)}, f32[16,256]{1,0:T(8,128)S(1)}, f3...) custom-call(s32[2]{0:T(128)S(1)} %get-tuple-element.39.base, ...), custom_call_target="tpu_custom_call" | custom-call | flops 4000000000 | bytes 4194304 | tf_op jit(solution)/shard_map/second/pallas_call | solution.py:301
  49.1 3.2 %collective-permute-start.2 = (bf16[2,2,512,256]{3,2,1,0:T(8,128)(2,1)S(1)}, bf16[2,2,512,256]{3,2,1,0:T(8,128)(2,1)S(1)}, u32[]{:S(2)}, u32[]{:S(2)}) collective-permute-start(bf16[2,2,512,256]{3,2,1,0:T(8,128)(2,1)S(1)} %get-tuple-element.35), channel_id=1, source_target_pairs={{0,2},{2,0},{1,3},{3,1},{4,6},{6,4},{5,7},{7,5},{8,10},{10,8},{9,1... | collective-permute-start | bytes 3145736 | tf_op jit(solution)/shard_map/ppermute | solution.py:364
  52.3 2.3 %collective-permute-done.2.arrived = bf16[2,2,512,256]{3,2,1,0:T(8,128)(2,1)S(1)} collective-permute-done((bf16[2,2,512,256]{3,2,1,0:T(8,128)(2,1)S(1)}, bf16[2,2,512,256]{3,2,1,0:T(8,128)(2,1)S(1)}, u32[]{:S(2)}, u32[]{:S(2)}) %collective-permute-start.2) | collective-permute-done | bytes 1048608 | tf_op jit(solution)/shard_map/ppermute | solution.py:364
  54.6 0.0 copy-done.1
  54.6 7.8 %third.1 = (bf16[32,2,8,512]{3,2,1,0:T(8,128)(2,1)}, bf16[2,256,512]{2,1,0:T(8,128)(2,1)S(1)}) custom-call(s32[2]{0:T(128)S(1)} %get-tuple-element.38.base, bf16[2,256,1024]{2,1,0:T(8,128)(2,1)S(1)} %project.1.kv, bf16[512,512]{1,0:T(8,128)(2,1)S(1)} %copy-done.6, bf16[512,512]{1,0:T(8,128)(2,1)S(1)} %copy-done.1, bf16[512,512]{1,0:T(8,128)(2,1)S(1)} %copy-done.3, ...), custom_call_target="tpu_custom_call" | custom-call | flops 2000000000 | bytes 4194304 | tf_op jit(solution)/shard_map/third/pallas_call | solution.py:345
  62.4 7.7 %all-to-all-start.1 = ((bf16[64,8,512]{2,1,0:T(8,128)(2,1)}), bf16[64,8,512]{2,1,0:T(8,128)(2,1)S(1)}, u32[]{:S(2)}, u32[]{:S(2)}) async-start(bf16[64,8,512]{2,1,0:T(8,128)(2,1)} %bitcast.5), calls=%async_computation.1 | async-start | bytes 1048576 | tf_op jit(solution)/shard_map/all_to_all | solution.py:395
  70.0 2.5 %collective-permute-start.3 = (bf16[2,256,512]{2,1,0:T(8,128)(2,1)S(1)}, bf16[2,256,512]{2,1,0:T(8,128)(2,1)S(1)}, u32[]{:S(2)}, u32[]{:S(2)}) collective-permute-start(bf16[2,256,512]{2,1,0:T(8,128)(2,1)S(1)} %get-tuple-element.37), channel_id=1, source_target_pairs={{0,1},{1,0},{2,3},{3,2},{4,5},{5,4},{6,7},{7,6},{8,9},{9,8},{10,11... | collective-permute-start | bytes 1572872 | tf_op jit(solution)/shard_map/ppermute | solution.py:364
  72.6 17.6 %collective-permute-done.3 = bf16[2,256,512]{2,1,0:T(8,128)(2,1)S(1)} collective-permute-done((bf16[2,256,512]{2,1,0:T(8,128)(2,1)S(1)}, bf16[2,256,512]{2,1,0:T(8,128)(2,1)S(1)}, u32[]{:S(2)}, u32[]{:S(2)}) %collective-permute-start.3) | collective-permute-done | bytes 524320 | tf_op jit(solution)/shard_map/ppermute | solution.py:364
  90.2 1.1 %add_multiply_fusion = f32[2,256,512]{2,1,0:T(8,128)} fusion(bf16[2,256,512]{2,1,0:T(8,128)(2,1)S(1)} %collective-permute-done.3, bf16[2,256,512]{2,1,0:T(8,128)(2,1)S(1)} %get-tuple-element.37), kind=kLoop, calls=%fused_computation | loop fusion | flops 1048576 | bytes 2097152 | tf_op jit(solution)/shard_map/mul | solution.py:394
  91.4 0.0 all-to-all-done.1
  91.4 0.1 convert_reduce_fusion
  91.5 0.6 broadcast_multiply_fusion
  (10 shorter events, 0.0 us)
Async XLA Ops:
  0.6 1.0 %copy-start = (bf16[512,512]{1,0:T(8,128)(2,1)S(1)}, bf16[512,512]{1,0:T(8,128)(2,1)}, u32[]{:S(2)}) copy-start(bf16[512,512]{1,0:T(8,128)(2,1)} %w_key.3) | copy-start | bytes 1572868
  1.7 1.0 %copy-start.2 = (bf16[512,512]{1,0:T(8,128)(2,1)S(1)}, bf16[512,512]{1,0:T(8,128)(2,1)}, u32[]{:S(2)}) copy-start(bf16[512,512]{1,0:T(8,128)(2,1)} %w_value.3) | copy-start | bytes 1572868
  2.7 1.0 %copy-start.5 = (bf16[2,256,512]{2,1,0:T(8,128)(2,1)S(1)}, bf16[2,256,512]{2,1,0:T(8,128)(2,1)}, u32[]{:S(2)}) copy-start(bf16[2,256,512]{2,1,0:T(8,128)(2,1)} %tokens.1) | copy-start | bytes 1572868
  3.8 4.0 %copy-start.8 = (s32[8]{0:T(128)S(1)}, s32[8]{0:T(128)}, u32[]{:S(2)}) copy-start(s32[8]{0:T(128)} %param.9) | copy-start | bytes 100
  3.8 4.1 %copy-start.7 = (bf16[8,512]{1,0:T(8,128)(2,1)S(1)}, bf16[8,512]{1,0:T(8,128)(2,1)}, u32[]{:S(2)}) copy-start(bf16[8,512]{1,0:T(8,128)(2,1)} %param.8) | copy-start | bytes 24580
  3.8 25.6 %copy-start.4 = (bf16[512,512]{1,0:T(8,128)(2,1)S(1)}, bf16[512,512]{1,0:T(8,128)(2,1)}, u32[]{:S(2)}) copy-start(bf16[512,512]{1,0:T(8,128)(2,1)} %w_out.5) | copy-start | bytes 1572868
  3.8 25.9 %copy-start.6 = (bf16[512,512]{1,0:T(8,128)(2,1)S(1)}, bf16[512,512]{1,0:T(8,128)(2,1)}, u32[]{:S(2)}) copy-start(bf16[512,512]{1,0:T(8,128)(2,1)} %w_query.5) | copy-start | bytes 1572868
  4.5 31.6 %collective-permute-start.1 = (bf16[2,256,1024]{2,1,0:T(8,128)(2,1)S(1)}, bf16[2,256,1024]{2,1,0:T(8,128)(2,1)}, u32[]{:S(2)}, u32[]{:S(2)}) collective-permute-start(bf16[2,256,1024]{2,1,0:T(8,128)(2,1)S(1)} %project.1.kv), channel_id=1, source_target_pairs={{0,2},{2,0},{1,3},{3,1},{4,6},{6,4},{5,7},{7,5},{8,10},{10,8},{9,1... | collective-permute-start | bytes 3145736 | tf_op jit(solution)/shard_map/ppermute | solution.py:364
  28.2 7.9 %collective-permute-start = (bf16[256,640]{1,0:T(8,128)(2,1)S(1)}, bf16[256,640]{1,0:T(8,128)(2,1)S(1)}, u32[]{:S(2)}, u32[]{:S(2)}) collective-permute-start(bf16[256,640]{1,0:T(8,128)(2,1)S(1)} %bitcast.9), channel_id=1, source_target_pairs={{0,4},{4,0},{1,5},{5,1},{2,6},{6,2},{3,7},{7,3},{8,12},{12,8},{9,1... | collective-permute-start | bytes 983048 | tf_op jit(solution)/shard_map/ppermute | solution.py:364
  36.1 18.5 %copy-start.1 = (bf16[512,512]{1,0:T(8,128)(2,1)S(1)}, bf16[512,512]{1,0:T(8,128)(2,1)}, u32[]{:S(2)}) copy-start(bf16[512,512]{1,0:T(8,128)(2,1)} %w_key.3) | copy-start | bytes 1572868
  36.1 18.5 %copy-start.3 = (bf16[512,512]{1,0:T(8,128)(2,1)S(1)}, bf16[512,512]{1,0:T(8,128)(2,1)}, u32[]{:S(2)}) copy-start(bf16[512,512]{1,0:T(8,128)(2,1)} %w_value.3) | copy-start | bytes 1572868
  49.1 5.5 %collective-permute-start.2 = (bf16[2,2,512,256]{3,2,1,0:T(8,128)(2,1)S(1)}, bf16[2,2,512,256]{3,2,1,0:T(8,128)(2,1)S(1)}, u32[]{:S(2)}, u32[]{:S(2)}) collective-permute-start(bf16[2,2,512,256]{3,2,1,0:T(8,128)(2,1)S(1)} %get-tuple-element.35), channel_id=1, source_target_pairs={{0,2},{2,0},{1,3},{3,1},{4,6},{6,4},{5,7},{7,5},{8,10},{10,8},{9,1... | collective-permute-start | bytes 3145736 | tf_op jit(solution)/shard_map/ppermute | solution.py:364
  62.4 29.0 %all-to-all-start.1 = ((bf16[64,8,512]{2,1,0:T(8,128)(2,1)}), bf16[64,8,512]{2,1,0:T(8,128)(2,1)S(1)}, u32[]{:S(2)}, u32[]{:S(2)}) async-start(bf16[64,8,512]{2,1,0:T(8,128)(2,1)} %bitcast.5), calls=%async_computation.1 | async-start | bytes 1048576 | tf_op jit(solution)/shard_map/all_to_all | solution.py:395
  70.0 20.2 %collective-permute-start.3 = (bf16[2,256,512]{2,1,0:T(8,128)(2,1)S(1)}, bf16[2,256,512]{2,1,0:T(8,128)(2,1)S(1)}, u32[]{:S(2)}, u32[]{:S(2)}) collective-permute-start(bf16[2,256,512]{2,1,0:T(8,128)(2,1)S(1)} %get-tuple-element.37), channel_id=1, source_target_pairs={{0,1},{1,0},{2,3},{3,2},{4,5},{5,4},{6,7},{7,6},{8,9},{9,8},{10,11... | collective-permute-start | bytes 1572872 | tf_op jit(solution)/shard_map/ppermute | solution.py:364
